TPU v7x, 1024 devices: a whole 4x8x16 slice. The times are simulated.
1024 devices in a mesh: section: 32 (over x_hi, z), tp: 8 (over y), dp: 4 (over x_lo, core).
Axes of the slice: x: 4 (x_hi: 2, x_lo: 2; x = x_hi * 2 + x_lo), y: 8, z: 16, core: 2. Of those that a mesh axis runs over, the one named last changes fastest.
Arguments:
- incoming: bfloat16 [32, 32, 128, 2304], P('section', ('dp', 'tp')), parts along dimension 1, may hold values from -6 to 6
- fresh_rows: bfloat16 [6, 32, 128, 2304], P(None, ('dp', 'tp')), parts along dimension 1, may hold values from -6 to 6
- entry_order: int32 [24], P('dp'), parts along dimension 0, may hold values from 0 to 5, each once
- flight_lengths: int32 [32, 32], P('section', 'dp'), parts along dimension 1, may hold values from 16 to 128
- pre_gain: float32 [32, 2304], P('section'), may hold values from 0.1 to 1.9
- post_gain: float32 [32, 2304], P('section'), may hold values from 0.1 to 1.9
- w_query: bfloat16 [32, 2304, 2048], P('section', None, 'tp'), may hold values from -0.125 to 0.125
- key_weight: bfloat16 [32, 2304, 1024], P('section', None, 'tp'), may hold values from -0.125 to 0.125
- value_weight: bfloat16 [32, 2304, 1024], P('section', None, 'tp'), may hold values from -0.125 to 0.125
- w_out: bfloat16 [32, 2048, 2304], P('section', 'tp'), may hold values from -0.125 to 0.125
Outputs:
- produced: bfloat16 [32, 32, 128, 2304], P('section', ('dp', 'tp')), parts along dimension 1
- advanced: bfloat16 [32, 32, 128, 2304], P('section', ('dp', 'tp')), parts along dimension 1
There are 4 independent parts, one for each index of `dp`. A program takes and returns all parts, laid end to end along the dimension named above; an argument that names none is the same for every part. Nothing has to cross between parts.
Inputs may be any that keep to these rules, and one draw needn't show every extreme that they name: `entry_order`: each waiting microbatch appears once.
All inputs are finite; a program needn't handle non-finite values.
Results may differ from a plain program's by a relative error of at most 0.012.
Values may be sent and summed in bfloat16 or wider, within the bound.
A program may use at most 64 MiB of HBM per device.

v0:
```python
import jax
import jax.numpy as jnp
from jax import lax
from jax.sharding import PartitionSpec as P

HEAD_WIDTH = 128


EPSILON = 1e-06
SOFT_CAP = 50.0
QUERY_SCALE = 144.0 ** (-0.5)


def shifted(block, axis, distance):
    devices = range(lax.axis_size(axis))
    route = [(i - distance, i) for i in devices if i - distance in devices]
    return lax.ppermute(block, axis, route)


def normalize(values, gain):
    return values * lax.rsqrt(jnp.mean(values * values, -1, keepdims=True) + EPSILON) * gain


def apply_rotary(values, token_positions):
    half = values.shape[-1] // 2
    freq = 10000.0 ** (-2.0 * jnp.arange(half).astype(jnp.float32) / values.shape[-1])
    angle = token_positions[:, None].astype(jnp.float32) * freq[None, :]
    cosine = jnp.cos(angle)[:, None, :]
    sine = jnp.sin(angle)[:, None, :]
    first = values[..., :half]
    second = values[..., half:]
    return jnp.concatenate([first * cosine - second * sine, second * cosine + first * sine], -1)


def layer(held, lengths, gain_before, gain_after, w_query, key_weight, value_weight, w_out):
    seq_len = held.shape[1]
    width = held.shape[2]
    own_rows = held.shape[0] * seq_len
    flat = held.reshape(own_rows, width)
    widened = flat.astype(jnp.float32)
    local_query = w_query.shape[1] // HEAD_WIDTH
    local_kv = key_weight.shape[1] // HEAD_WIDTH
    query_cols = local_query * HEAD_WIDTH
    kv_cols = local_kv * HEAD_WIDTH
    normalized_input = normalize(
        lax.all_gather(flat, "tp", axis=0, tiled=True).astype(jnp.float32), gain_before
    ).astype(jnp.bfloat16)
    count = normalized_input.shape[0]
    token_positions = jnp.arange(count) % seq_len
    query_matrix = jnp.dot(normalized_input, w_query, preferred_element_type=jnp.float32).reshape(
        count, local_query, HEAD_WIDTH
    )
    projected_keys = jnp.dot(
        normalized_input, key_weight, preferred_element_type=jnp.float32
    ).reshape(count, local_kv, HEAD_WIDTH)
    projected_values = jnp.dot(normalized_input, value_weight, preferred_element_type=jnp.float32)
    projected = jnp.concatenate(
        [
            apply_rotary(query_matrix, token_positions).reshape(count, query_cols),
            apply_rotary(projected_keys, token_positions).reshape(count, kv_cols),
            projected_values,
        ],
        1,
    ).astype(jnp.bfloat16)
    total_rows = projected.shape[0]
    batch = total_rows // seq_len
    group = local_query // local_kv
    query_matrix = projected[:, :query_cols].reshape(batch, seq_len, local_kv, group, HEAD_WIDTH)
    projected_keys = projected[:, query_cols : query_cols + kv_cols].reshape(
        batch, seq_len, local_kv, HEAD_WIDTH
    )
    projected_values = projected[:, query_cols + kv_cols :].reshape(
        batch, seq_len, local_kv, HEAD_WIDTH
    )
    scores = (
        jnp.einsum(
            "bqkgd,bskd->bkgqs", query_matrix, projected_keys, preferred_element_type=jnp.float32
        )
        * QUERY_SCALE
    )
    capped = SOFT_CAP * jnp.tanh(scores / SOFT_CAP)
    position = jnp.arange(seq_len)
    causal = position[None, :] <= position[:, None]
    allowed = causal[None, :, :] & (position[None, None, :] < lengths[:, None, None])
    raised = jnp.where(allowed[:, None, None, :, :], jnp.exp(capped), jnp.float32(0.0))
    probs = (raised / jnp.sum(raised, -1, keepdims=True)).astype(jnp.bfloat16)
    mixed = jnp.einsum(
        "bkgqs,bskd->bqkgd", probs, projected_values, preferred_element_type=jnp.float32
    ).astype(jnp.bfloat16)
    mixed_flat = mixed.reshape(total_rows, query_cols)
    branch_sum = lax.psum_scatter(
        jnp.dot(mixed_flat, w_out, preferred_element_type=jnp.float32).astype(jnp.bfloat16),
        "tp",
        scatter_dimension=0,
        tiled=True,
    ).astype(jnp.float32)
    return (widened + normalize(branch_sum, gain_after)).astype(jnp.bfloat16).reshape(held.shape)


def shards(
    incoming,
    fresh_rows,
    entry_order,
    flight_lengths,
    pre_gain,
    post_gain,
    w_query,
    key_weight,
    value_weight,
    w_out,
):
    section_index = lax.axis_index("section")
    produced = layer(
        incoming[0],
        flight_lengths[0],
        pre_gain[0],
        post_gain[0],
        w_query[0],
        key_weight[0],
        value_weight[0],
        w_out[0],
    )
    received = shifted(produced, "section", 1)
    entering = lax.dynamic_index_in_dim(fresh_rows, entry_order[0], 0, keepdims=False)
    advanced = jnp.where(section_index == 0, entering, received)
    return (produced[None], advanced[None])


def solution(mesh):
    in_specs = (
        P("section", ("dp", "tp"), None, None),
        P(None, ("dp", "tp"), None, None),
        P("dp"),
        P("section", "dp"),
        P("section", None),
        P("section", None),
        P("section", None, "tp"),
        P("section", None, "tp"),
        P("section", None, "tp"),
        P("section", "tp", None),
    )
    out_specs = (P("section", ("dp", "tp"), None, None), P("section", ("dp", "tp"), None, None))
    return jax.shard_map(shards, mesh=mesh, in_specs=in_specs, out_specs=out_specs, check_vma=False)
```

profile of v0, /device:TPU:6, one launch (start us, length us, event | category | flops | bytes accessed | tf_op | source)
XLA Modules:
  0.0 205.5 jit_solution(7365288358224885538)
XLA Ops:
  7.2 0.0 copy-start
  7.2 0.0 all-gather.3.cloned.1.call-start
  7.2 0.7 all-gather.3.cloned.1.call-update
  7.9 0.0 reduce-scatter.2.cloned.1.call-start
  8.0 1.6 copy.29
  9.5 0.7 reduce.1
  10.3 0.7 iota_compare_fusion.1
  11.0 0.2 broadcast_and_fusion
  11.3 1.0 multiply_cosine_fusion
  12.2 73.4 %all-gather.3.cloned.1.call-done = bf16[1,1,1024,2304]{3,2,1,0:T(8,128)(2,1)} async-done(((bf16[1,1,128,2304]{3,2,1,0:T(8,128)(2,1)}), bf16[1,1,1024,2304]{3,2,1,0:T(8,128)(2,1)}) %all-gather.3.cloned.1.call-update) | async-done | bytes 4718608 | tf_op jit(solution)/shard_map/all_gather | solution.py:46
  85.7 3.5 %fusion = f32[1024]{0:T(1024)S(1)} fusion(bf16[1,1,1024,2304]{3,2,1,0:T(8,128)(2,1)} %all-gather.3.cloned.1.call-done), kind=kLoop, calls=%fused_computation.2 | loop fusion | flops 7076864 | bytes 4722688 | tf_op jit(solution)/shard_map/reduce_sum | solution.py:21
  89.2 0.3 copy-done.1
  89.5 2.8 %convolution_bitcast_fusion = f32[1024,1,128]{0,2,1:T(8,128)S(1)} fusion(bf16[1,2304,128]{2,1,0:T(8,128)(2,1)} %param.17, bf16[1,1,1024,2304]{3,2,1,0:T(8,128)(2,1)S(1)} %copy-done.1, f32[2304]{0:T(1024)S(1)} %reduce.1, f32[1024]{0:T(1024)S(1)} %add_rsqrt_fusion), kind=kOutput, calls=%fused_computation.18 | convolution fusion | flops 613416960 | bytes 5846016 | tf_op jit(solution)/shard_map/dot_general | solution.py:53
  92.2 1.2 fusion.29
  93.4 0.2 copy.28
  93.6 4.0 %fusion.3 = f32[1024,2,128]{0,2,1:T(8,128)S(1)} fusion(bf16[2,128,2304]{2,1,0:T(8,128)(2,1)S(1)} %bitcast.93, bf16[1,1,1024,2304]{3,2,1,0:T(8,128)(2,1)} %all-gather.3.cloned.1.call-done, f32[2304]{0:T(1024)S(1)} %reduce.1, f32[1024]{0:T(1024)S(1)} %add_rsqrt_fusion), kind=kOutput, calls=%fused_computation.6 | convolution fusion | flops 1217396736 | bytes 6960128 | tf_op jit(solution)/shard_map/dot_general | solution.py:50
  97.6 0.0 copy-start.5
  97.6 0.2 subtract_convert_fusion
  97.8 0.5 fusion.41
  98.3 0.4 copy-done.5
  98.7 1.5 convolution_convert_fusion.2
  100.2 0.4 fusion.10
  100.6 0.3 copy.22
  100.9 0.0 copy-start.3
  100.9 3.6 %convolution_convert_fusion = bf16[1024,2304]{1,0:T(8,128)(2,1)} fusion(bf16[1,256,2304]{2,1,0:T(8,128)(2,1)S(1)} %copy-done, bf16[32,8,8,128]{3,2,1,0:T(8,128)(2,1)S(1)} %bitcast.91), kind=kOutput, calls=%fused_computation.5 | convolution fusion | flops 1210318848 | bytes 6422528 | tf_op jit(solution)/shard_map/dot_general | solution.py:92
  104.5 0.0 reduce-scatter.2.cloned.1.call-update
  104.6 67.3 %reduce-scatter.2.cloned.1.call-done = bf16[128,2304]{1,0:T(8,128)(2,1)} async-done(((bf16[1024,2304]{1,0:T(8,128)(2,1)}), bf16[128,2304]{1,0:T(8,128)(2,1)}) %reduce-scatter.2.cloned.1.call-update) | async-done | bytes 589840 | tf_op jit(solution)/shard_map/reduce_scatter | solution.py:91
  171.9 1.3 fusion.11
  173.1 2.2 %fusion.36 = (bf16[1,128,2304]{2,1,0:T(8,128)(2,1)S(1)}, bf16[1,1,128,2304]{3,2,1,0:T(8,128)(2,1)}) fusion(f32[2304]{0:T(1024)S(1)} %reduce.2, f32[128]{0:T(128)S(1)} %add_rsqrt_fusion.1, bf16[128,2304]{1,0:T(8,128)(2,1)} %reduce-scatter.2.cloned.1.call-done, bf16[1,1,128,2304]{3,2,1,0:T(8,128)(2,1)S(1)} %copy-done.2), kind=kLoop, calls=%fused_computation.63 | loop fusion | flops 1769472 | bytes 2369024 | tf_op jit(solution)/shard_map/reshape | solution.py:97
  175.3 3.5 %collective-permute-start = (bf16[1,128,2304]{2,1,0:T(8,128)(2,1)S(1)}, bf16[1,128,2304]{2,1,0:T(8,128)(2,1)S(1)}, u32[]{:S(2)}, u32[]{:S(2)}) collective-permute-start(bf16[1,128,2304]{2,1,0:T(8,128)(2,1)S(1)} %get-tuple-element.4), channel_id=1, source_target_pairs={{0,32},{32,64},{64,96},{96,128},{128,160},{160,192},{192,224},{224... | collective-permute-start | bytes 1769480 | tf_op jit(solution)/shard_map/ppermute | solution.py:17
  179.0 17.8 %collective-permute-done = bf16[1,128,2304]{2,1,0:T(8,128)(2,1)S(1)} collective-permute-done((bf16[1,128,2304]{2,1,0:T(8,128)(2,1)S(1)}, bf16[1,128,2304]{2,1,0:T(8,128)(2,1)S(1)}, u32[]{:S(2)}, u32[]{:S(2)}) %collective-permute-start) | collective-permute-done | bytes 589856 | tf_op jit(solution)/shard_map/ppermute | solution.py:17
  196.8 1.9 fusion.16
  (19 shorter events, 0.1 us)
Async XLA Ops:
  7.2 93.7 %copy-start = (bf16[1,256,2304]{2,1,0:T(8,128)(2,1)S(1)}, bf16[1,256,2304]{2,1,0:T(8,128)(2,1)}, u32[]{:S(2)}) copy-start(bf16[1,256,2304]{2,1,0:T(8,128)(2,1)} %param.19) | copy-start | bytes 3538948
  7.2 78.5 %all-gather.3.cloned.1.call-start = ((), (), s32[]{:S(2)}) async-start(), calls=%async_computation.2 | async-start | bytes 5308416 | tf_op jit(solution)/shard_map/all_gather | solution.py:46
  7.9 164.0 %reduce-scatter.2.cloned.1.call-start = ((), (), s32[]{:S(2)}) async-start(), calls=%async_computation.1 | async-start | bytes 5308416 | tf_op jit(solution)/shard_map/reduce_scatter | solution.py:91
  85.7 3.8 %copy-start.1 = (bf16[1,1,1024,2304]{3,2,1,0:T(8,128)(2,1)S(1)}, bf16[1,1,1024,2304]{3,2,1,0:T(8,128)(2,1)}, u32[]{:S(2)}) copy-start(bf16[1,1,1024,2304]{3,2,1,0:T(8,128)(2,1)} %all-gather.3.cloned.1.call-done) | copy-start | bytes 14155780
  93.6 4.7 %slice-start = ((s8[4718592]{0:T(1024)(128)(4,1)}), s8[4194304]{0:T(1024)(128)(4,1)S(1)}, s32[]{:S(2)}) async-start(s8[4718592]{0:T(1024)(128)(4,1)} %bitcast.89), calls=%async_computation.3 | async-start | bytes 8388608
  93.6 4.7 %slice-start.1 = ((s8[4718592]{0:T(1024)(128)(4,1)}), s8[524288]{0:T(1024)(128)(4,1)S(1)}, s32[]{:S(2)}) async-start(s8[4718592]{0:T(1024)(128)(4,1)} %bitcast.89), calls=%async_computation.4 | async-start | bytes 1048576
  97.6 1.1 copy-start.5
  100.9 3.6 %copy-start.3 = (f32[1,2304]{1,0:T(1,128)S(1)}, f32[1,2304]{1,0:T(1,128)}, u32[]{:S(2)}) copy-start(f32[1,2304]{1,0:T(1,128)} %param.15) | copy-start | bytes 27652
  100.9 72.2 %copy-start.2 = (bf16[1,1,128,2304]{3,2,1,0:T(8,128)(2,1)S(1)}, bf16[1,1,128,2304]{3,2,1,0:T(8,128)(2,1)}, u32[]{:S(2)}) copy-start(bf16[1,1,128,2304]{3,2,1,0:T(8,128)(2,1)} %param.10) | copy-start | bytes 1769476
  104.5 74.4 %copy-start.4 = (s32[6]{0:T(128)S(1)}, s32[6]{0:T(128)}, u32[]{:S(2)}) copy-start(s32[6]{0:T(128)} %param.12) | copy-start | bytes 76
  175.3 21.4 %collective-permute-start = (bf16[1,128,2304]{2,1,0:T(8,128)(2,1)S(1)}, bf16[1,128,2304]{2,1,0:T(8,128)(2,1)S(1)}, u32[]{:S(2)}, u32[]{:S(2)}) collective-permute-start(bf16[1,128,2304]{2,1,0:T(8,128)(2,1)S(1)} %get-tuple-element.4), channel_id=1, source_target_pairs={{0,32},{32,64},{64,96},{96,128},{128,160},{160,192},{192,224},{224... | collective-permute-start | bytes 1769480 | tf_op jit(solution)/shard_map/ppermute | solution.py:17
Sparse Core Ops, SparseCore 0:
  10.6 75.0 all-gather.2
  104.6 67.1 reduce-scatter.1
where the time goes:
time: 206 us
  waiting for transfers between devices  159 us (77%)
  between operations  14.4 us (7%)
  other arithmetic  12.9 us (6%)
  matrix products  12.7 us (6%)
  starting transfers between devices  3.62 us (2%)
  local copies, waits for them, and re-layouts  2.76 us (1%)
    all_gather x1, waiting for transfers between devices, layer(): lax.all_gather(flat, 'tp', axis=0, tiled=True).astype(jnp.float32)  73.4 us
    reduce_scatter x1, waiting for transfers between devices, layer(): lax.psum_scatter(jnp.dot(mixed_flat, w_out, preferred_element_type=jnp.fl...  67.3 us
    ppermute x1, waiting for transfers between devices, shifted(): return lax.ppermute(block, axis, route)  17.8 us
    reduce_sum x2, other arithmetic, normalize(): jnp.mean(values * values, -1, keepdims=True) + EPSILON  4.74 us
  transfers between devices with their start and end apart: 3, of which 3 were waited for; matrix products, arithmetic and copies ran while one was open for 2% of the time, Pallas kernels for 0%

commit v1 on v0

v1 whole, which is shorter than its diff:
```python
import functools

import jax
import jax.numpy as jnp
import numpy as np
from jax import lax
from jax.experimental import pallas as pl
from jax.experimental.pallas import tpu as pltpu
from jax.sharding import PartitionSpec as P

HEAD_WIDTH = 128
EPSILON = 1e-06
SOFT_CAP = 50.0
QUERY_SCALE = 144.0 ** (-0.5)
MESH = pl.DeviceIdType.MESH
CHUNKS = 4

STEPS = [
    ("A", 0, 0), ("D", 0), ("A", 1, 0),
    ("U", 0, 0), ("A", 0, 1), ("U", 1, 0), ("U", 0, 1),
    ("D", 1), ("A", 1, 1), ("U", 1, 1),
    ("A", 0, 2), ("U", 0, 2), ("D", 2), ("X", 0), ("A", 1, 2), ("U", 1, 2),
    ("A", 0, 3), ("A", 2, 0), ("U", 0, 3), ("D", 3), ("X", 1), ("A", 1, 3), ("U", 1, 3), ("A", 3, 0),
    ("A", 0, 4), ("U", 0, 4), ("D", 4), ("A", 1, 4), ("U", 1, 4), ("U", 2, 0), ("U", 3, 0),
    ("A", 2, 1), ("U", 2, 1), ("A", 3, 1), ("X", 2), ("U", 3, 1), ("A", 2, 2), ("X", 3),
    ("U", 2, 2), ("A", 3, 2), ("U", 3, 2), ("W",), ("O", 0), ("A", 2, 3), ("U", 2, 3), ("O", 1), ("A", 3, 3), ("U", 3, 3),
    ("A", 2, 4), ("U", 2, 4), ("A", 3, 4), ("U", 3, 4), ("O", 2), ("O", 3),
]


def kernel(
    n_section, lens, x, gain_before, gain_after, cosine, sine, wq, wk, wv, wo,
    produced, received,
    xg, wqkv, wout, keys, values, normed, outgoing, mixed, branch, made, g1, g2, cs, sn,
    a_send, a_recv, d_send, d_recv, x_send, x_recv, e_send, e_recv, f_send, f_recv, c_send, c_recv,
    z_send, z_recv, l_sem, o_sem,
):
    n_tp = wout.shape[0]
    section = lax.axis_index("section")
    t = lax.axis_index("tp")
    dp = lax.axis_index("dp")
    seq, width = x.shape
    rows = seq // CHUNKS
    group = wo.shape[0]
    quarter = group // 4
    kv = wk.shape[1]
    other_core = dp + 1 - 2 * lax.rem(dp, 2)
    beside = lax.rem(dp + 2, 4)

    def at_tp(distance):
        return lax.rem(t + n_tp + distance, n_tp)

    sources = (x, wq, wk, wv, wo, gain_before, gain_after, cosine, sine)
    targets = (
        xg.at[t], wqkv.at[:, :group], wqkv.at[:, group:group + kv], wqkv.at[:, group + kv:], wout.at[t], g1, g2, cs, sn,
    )
    local = [pltpu.make_async_copy(s, d, l_sem.at[i]) for i, (s, d) in enumerate(zip(sources, targets))]
    for copy in local:
        copy.start()

    barrier = pltpu.get_barrier_semaphore()
    for distance in range(1, n_tp):
        pl.semaphore_signal(barrier, inc=1, device_id={"tp": at_tp(distance)}, device_id_type=MESH)
    pl.semaphore_signal(barrier, inc=1, device_id={"dp": other_core}, device_id_type=MESH)
    pl.semaphore_signal(barrier, inc=1, device_id={"dp": beside}, device_id_type=MESH)

    for distance in (1, n_section - 1):
        pl.semaphore_signal(
            barrier, inc=1, device_id={"section": lax.rem(section + distance, n_section)}, device_id_type=MESH
        )
    pl.semaphore_wait(barrier, n_tp + 3)

    pending = []

    def remote(src, dst, send, recv, device):
        return pltpu.make_async_remote_copy(
            src_ref=src, dst_ref=dst, send_sem=send, recv_sem=recv, device_id=device, device_id_type=MESH
        )

    def start(copy):
        copy.start()
        pending.append(copy)

    def ring_rows(way, c, h):
        if h < 3:
            return pl.ds(c * rows, rows)
        return pl.ds(c * rows + way * (rows // 2), rows // 2)

    def ring(way, c, h, arriving):
        sign = 1 if way == 0 else -1
        block = at_tp(-sign * (h + 1 if arriving else h))
        part = xg.at[block, ring_rows(way, c, h)]
        src = x.at[ring_rows(way, c, h)] if h == 0 and not arriving else part
        return remote(src, part, a_send.at[way, c, h], a_recv.at[way, c, h], {"tp": at_tp(sign)})

    def weight_rows(who, way, h):
        if h < 3:
            return pl.ds(who * quarter, quarter)
        return pl.ds(who * quarter + way * (quarter // 2), quarter // 2)

    def weight_part(who, way, h, arriving):
        sign = 1 if way == 0 else -1
        return wout.at[at_tp(-sign * (h + 1 if arriving else h)), weight_rows(who, way, h)]

    def weight_ring(way, h, arriving):
        sign = 1 if way == 0 else -1
        part = weight_part(dp, way, h, arriving)
        src = wo.at[weight_rows(dp, way, h)] if h == 0 and not arriving else part
        return remote(src, part, d_send.at[way, h], d_recv.at[way, h], {"tp": at_tp(sign)})

    def weight_beside(who, way, h):
        part = weight_part(who, way, h, True)
        return remote(part, part, x_send.at[way, h], x_recv.at[way, h], {"dp": beside})

    def weight_core(who, way, h, second):
        part = weight_part(who, way, h, True)
        sems = (f_send, f_recv) if second else (e_send, e_recv)
        return remote(part, part, sems[0].at[way, h], sems[1].at[way, h], {"dp": other_core})

    def exchange(c, r):
        return remote(outgoing.at[c, r], mixed.at[c, t], c_send.at[c, r], c_recv.at[c, r], {"tp": at_tp(r)})

    def exchange_arriving(c, r):
        part = mixed.at[c, at_tp(-r)]
        return remote(part, part, c_send.at[c, r], c_recv.at[c, r], {"tp": at_tp(r)})

    late = []

    def flush():
        while late:
            start(late.pop(0))

    def attend(c, g):
        if g == 0:
            blocks = [(t, None)]
        elif g == n_tp // 2:
            blocks = [(at_tp(g), g)]
        else:
            blocks = [(at_tp(-g), n_tp - g), (at_tp(g), g)]
        gain = g1[...]
        for i, (block, _) in enumerate(blocks):
            row = x_rows = xg[block, c * rows:(c + 1) * rows].astype(jnp.float32)
            scale = lax.rsqrt(jnp.mean(row * row, -1, keepdims=True) + EPSILON)
            normed[i * rows:(i + 1) * rows] = (x_rows * scale * gain).astype(jnp.bfloat16)
        total = len(blocks) * rows
        projected = jnp.dot(normed[:total], wqkv[...], preferred_element_type=jnp.float32)
        cos_part = cs[c * rows:(c + 1) * rows]
        sin_part = sn[c * rows:(c + 1) * rows]

        def rotate(part):
            return (part * cos_part + pltpu.roll(part, HEAD_WIDTH // 2, 1) * sin_part).astype(jnp.bfloat16)

        heads = group // HEAD_WIDTH
        query_at = lax.broadcasted_iota(jnp.int32, (heads * rows, seq), 0) % rows + c * rows
        key_at = lax.broadcasted_iota(jnp.int32, (heads * rows, seq), 1)
        for i, (block, r) in enumerate(blocks):
            part = projected[i * rows:(i + 1) * rows]
            query = jnp.concatenate(
                [rotate(part[:, h * HEAD_WIDTH:(h + 1) * HEAD_WIDTH]) for h in range(heads)], 0
            )
            keys[block, c * rows:(c + 1) * rows] = rotate(part[:, group:group + kv])
            values[block, c * rows:(c + 1) * rows] = part[:, group + kv:].astype(jnp.bfloat16)
            scores = lax.dot_general(
                query, keys[block], (((1,), (1,)), ((), ())), preferred_element_type=jnp.float32
            )
            capped = SOFT_CAP * jnp.tanh(scores * (QUERY_SCALE / SOFT_CAP))
            allowed = (key_at <= query_at) & (key_at < lens[0, block])
            raised = jnp.where(allowed, jnp.exp(capped), 0.0)
            probs = (raised / jnp.sum(raised, -1, keepdims=True)).astype(jnp.bfloat16)
            out = jnp.dot(probs, values[block], preferred_element_type=jnp.float32).astype(jnp.bfloat16)
            for h in range(heads):
                piece = out[h * rows:(h + 1) * rows]
                if r is None:
                    mixed[c, t, :, h * HEAD_WIDTH:(h + 1) * HEAD_WIDTH] = piece
                else:
                    outgoing[c, r, :, h * HEAD_WIDTH:(h + 1) * HEAD_WIDTH] = piece
            if r is not None:
                late.append(exchange(c, r))

    def finish(c):
        for r in range(1, n_tp):
            exchange_arriving(c, r).wait_recv()
        tile = 256
        square = jnp.zeros((rows, 1), jnp.float32)
        for n in range(width // tile):
            cols = slice(n * tile, (n + 1) * tile)
            acc = jnp.zeros((rows, tile), jnp.float32)
            for j in range(n_tp):
                acc += jnp.dot(mixed[c, j], wout[j, :, cols], preferred_element_type=jnp.float32)
            branch[:, cols] = acc
            square += jnp.sum(acc * acc, -1, keepdims=True)
        scale = lax.rsqrt(square / width + EPSILON)
        part = slice(c * rows, (c + 1) * rows)
        held = xg[t, part].astype(jnp.float32)
        made[part] = (held + branch[...] * scale * g2[...]).astype(jnp.bfloat16)
        copy = pltpu.make_async_copy(made.at[part], produced.at[part], o_sem.at[c])
        copy.start()

        @pl.when(section < n_section - 1)
        def _():
            send_on(c).start()

    def send_on(c):
        part = slice(c * rows, (c + 1) * rows)
        return remote(made.at[part], received.at[part], z_send.at[c], z_recv.at[c], {"section": section + 1})

    ready = False
    for step in STEPS:
        kind = step[0]
        if kind == "A":
            _, c, h = step
            for way in (0, 1):
                if h > 0:
                    ring(way, c, h - 1, True).wait_recv()
                if h < 4:
                    start(ring(way, c, h, False))
            flush()
        elif kind == "D":
            h = step[1]
            for way in (0, 1):
                if h > 0:
                    weight_ring(way, h - 1, True).wait_recv()
                if h < 4:
                    start(weight_ring(way, h, False))
                if h > 0:
                    start(weight_beside(dp, way, h - 1))
                    start(weight_core(dp, way, h - 1, False))
            flush()
        elif kind == "X":
            h = step[1]
            for way in (0, 1):
                weight_beside(beside, way, h).wait_recv()
                start(weight_core(beside, way, h, True))
            flush()
        elif kind == "W":
            for h in range(4):
                for way in (0, 1):
                    weight_core(other_core, way, h, False).wait_recv()
                    weight_core(lax.rem(other_core + 2, 4), way, h, True).wait_recv()
        elif kind == "U":
            if not ready:
                keys[...] = jnp.zeros_like(keys)
                values[...] = jnp.zeros_like(values)
                for copy in local:
                    copy.wait()
                ready = True
            flush()
            attend(step[1], step[2])
        else:
            flush()
            finish(step[1])

    for copy in pending:
        copy.wait_send()
    for c in range(CHUNKS):
        part = slice(c * rows, (c + 1) * rows)
        pltpu.make_async_copy(made.at[part], produced.at[part], o_sem.at[c]).wait()

    @pl.when(section < n_section - 1)
    def _():
        for c in range(CHUNKS):
            send_on(c).wait_send()

    @pl.when(section > 0)
    def _():
        for c in range(CHUNKS):
            send_on(c).wait_recv()


def tables(seq):
    half = HEAD_WIDTH // 2
    freq = 10000.0 ** (-2.0 * np.arange(half) / HEAD_WIDTH)
    angle = np.arange(seq)[:, None] * freq[None, :]
    cosine, sine = np.cos(angle), np.sin(angle)
    return (
        np.concatenate([cosine, cosine], -1).astype(np.float32),
        np.concatenate([-sine, sine], -1).astype(np.float32),
    )


def shards(
    n_section, n_tp, incoming, fresh_rows, entry_order, flight_lengths, pre_gain, post_gain,
    w_query, key_weight, value_weight, w_out,
):
    held = incoming[0, 0]
    seq, width = held.shape
    rows = seq // CHUNKS
    wq, wk, wv, wo = w_query[0], key_weight[0], value_weight[0], w_out[0]
    group, kv = wq.shape[1], wk.shape[1]
    cosine, sine = tables(seq)
    hbm = pl.BlockSpec(memory_space=pl.ANY)
    bf16, f32 = jnp.bfloat16, jnp.float32
    dma = pltpu.SemaphoreType.DMA
    produced, received = pl.pallas_call(
        functools.partial(kernel, n_section),
        out_shape=[jax.ShapeDtypeStruct((seq, width), bf16)] * 2,
        in_specs=[pl.BlockSpec(memory_space=pltpu.SMEM)] + [hbm] * 9,
        out_specs=[hbm] * 2,
        scratch_shapes=[
            pltpu.VMEM((n_tp, seq, width), bf16),
            pltpu.VMEM((width, group + 2 * kv), bf16),
            pltpu.VMEM((n_tp, group, width), bf16),
            pltpu.VMEM((n_tp, seq, kv), bf16),
            pltpu.VMEM((n_tp, seq, kv), bf16),
            pltpu.VMEM((2 * rows, width), bf16),
            pltpu.VMEM((CHUNKS, n_tp, rows, group), bf16),
            pltpu.VMEM((CHUNKS, n_tp, rows, group), bf16),
            pltpu.VMEM((rows, width), f32),
            pltpu.VMEM((seq, width), bf16),
            pltpu.VMEM((1, width), f32),
            pltpu.VMEM((1, width), f32),
            pltpu.VMEM((seq, HEAD_WIDTH), f32),
            pltpu.VMEM((seq, HEAD_WIDTH), f32),
            dma((2, CHUNKS, 4)), dma((2, CHUNKS, 4)),
            dma((2, 4)), dma((2, 4)), dma((2, 4)), dma((2, 4)), dma((2, 4)), dma((2, 4)), dma((2, 4)), dma((2, 4)),
            dma((CHUNKS, n_tp)), dma((CHUNKS, n_tp)),
            dma((CHUNKS,)), dma((CHUNKS,)), dma((9,)), dma((CHUNKS,)),
        ],
        compiler_params=pltpu.CompilerParams(
            collective_id=0, has_side_effects=True, vmem_limit_bytes=40 * 1024 * 1024
        ),
        name="relay",
    )(
        flight_lengths, held, pre_gain, post_gain, jnp.asarray(cosine), jnp.asarray(sine), wq, wk, wv, wo,
    )
    entering = lax.dynamic_index_in_dim(fresh_rows, entry_order[0], 0, keepdims=False)[0]
    advanced = jnp.where(lax.axis_index("section") == 0, entering, received)
    return produced[None, None], advanced[None, None]


def solution(mesh):
    in_specs = (
        P("section", ("dp", "tp"), None, None),
        P(None, ("dp", "tp"), None, None),
        P("dp"),
        P("section", "dp"),
        P("section", None),
        P("section", None),
        P("section", None, "tp"),
        P("section", None, "tp"),
        P("section", None, "tp"),
        P("section", "tp", None),
    )
    out_specs = (P("section", ("dp", "tp"), None, None), P("section", ("dp", "tp"), None, None))
    return jax.shard_map(
        functools.partial(shards, mesh.shape["section"], mesh.shape["tp"]),
        mesh=mesh, in_specs=in_specs, out_specs=out_specs, check_vma=False,
    )
```

time: 206 us -> 132 us (0.64)
  waiting for transfers between devices: 159 us -> 0 us
  Pallas kernels: 0 us -> 116 us
  matrix products: 12.7 us -> 0 us
  between operations: 14.4 us -> 2.6 us
  other arithmetic: 12.9 us -> 1.95 us
  local copies, waits for them, and re-layouts: 2.76 us -> 10.3 us
  starting transfers between devices: 3.62 us -> 0 us
    pallas_call x0 -> x1, Pallas kernels: none -> 116 us  [shards(): pl.pallas_call(functools.partial(kernel, n_section), out_shape=[jax.Shape...]
    all_gather x1 -> x0, waiting for transfers between devices: 73.4 us -> none  [layer(): lax.all_gather(flat, 'tp', axis=0, tiled=True).astype(jnp.float32)]
    reduce_scatter x1 -> x0, waiting for transfers between devices: 67.3 us -> none  [layer(): lax.psum_scatter(jnp.dot(mixed_flat, w_out, preferred_element_type=jnp.fl...]
    ppermute x1 -> x0, waiting for transfers between devices: 17.8 us -> none  [shifted(): return lax.ppermute(block, axis, route)]
    dot_general x6 -> x0, matrix products: 12.7 us -> none  [the longest x1 3.98 us: layer(): jnp.dot(normalized_input, w_query, preferred_element_type=jnp.float32)]
    unnamed x16 -> x21, local copies, waits for them, and re-layouts: 0.68 us -> 10.3 us
    reduce_sum x2 -> x0, other arithmetic: 4.74 us -> none  [normalize(): jnp.mean(values * values, -1, keepdims=True) + EPSILON]
    ppermute x1 -> x0, starting transfers between devices: 3.54 us -> none  [shifted(): return lax.ppermute(block, axis, route)]
  transfers between devices with their start and end apart: 3 -> 0, of which waited for: 3 -> 0; matrix products, arithmetic and copies ran while one was open for 2% -> 0% of each run, Pallas kernels for 0% -> 0%
where the time goes in v1:
time: 132 us; the launch traced here: 131 us
  Pallas kernels  116 us (88%)
  local copies, waits for them, and re-layouts  10.3 us (8%)
  between operations  2.6 us (2%)
  other arithmetic  1.95 us (1%)
    pallas_call x1, Pallas kernels, shards(): pl.pallas_call(functools.partial(kernel, n_section), out_shape=[jax.Shape...  116 us
    unnamed x21, local copies, waits for them, and re-layouts  10.3 us

profile of v1, /device:TPU:6, one launch (start us, length us, event | category | flops | bytes accessed | tf_op | source)
XLA Modules:
  0.0 131.1 jit_solution(16645766507171111412)
XLA Ops:
  2.6 0.0 copy-start
  2.6 1.3 copy-done
  3.8 0.0 copy-start.1
  3.9 1.3 copy-done.1
  5.1 0.0 copy-start.2
  5.1 1.1 copy-done.2
  6.2 0.0 copy-start.3
  6.2 1.1 copy-done.3
  7.2 0.0 copy-start.4
  7.3 1.1 copy-done.4
  8.3 0.0 copy-start.5
  8.3 0.8 copy-done.5
  9.2 0.0 copy-start.6
  9.2 0.8 copy-done.6
  10.0 0.0 copy-start.7
  10.0 0.7 copy-done.7
  10.7 0.0 copy-start.8
  10.7 0.7 copy-done.8
  11.4 0.0 copy-start.9
  11.4 0.7 copy-done.9
  12.0 116.2 %relay.1 = (bf16[128,2304]{1,0:T(8,128)(2,1)S(1)}, bf16[128,2304]{1,0:T(8,128)(2,1)S(1)}) custom-call(s32[1,8]{1,0:T(1,128)S(1)} %copy-done.9, bf16[128,2304]{1,0:T(8,128)(2,1)S(1)} %bitcast.17, f32[1,2304]{1,0:T(1,128)S(1)} %copy-done.7, f32[1,2304]{1,0:T(1,128)S(1)} %copy-done.8, f32[128,128]{1,0:T(8,128)S(1)} %copy-done.6, f32[128,128]{1,0:T(8,128)S(1)} %copy-done.5, ...), custom_call_target="tpu_custom_call" | custom-call | tf_op jit(solution)/shard_map/relay/pallas_call | solution.py:294
  128.3 1.9 %fusion = bf16[1,1,128,2304]{3,2,1,0:T(8,128)(2,1)} fusion(bf16[128,2304]{1,0:T(8,128)(2,1)S(1)} %get-tuple-element.5, bf16[6,1,128,2304]{3,2,1,0:T(8,128)(2,1)} %param.13, s32[]{:T(128)S(6)} %select_n.13, pred[]{:T(512)S(6)} %eq.3), kind=kLoop, calls=%fused_computation.1 | loop fusion | flops 294912 | bytes 1769477 | tf_op jit(solution)/shard_map/broadcast_in_dim | solution.py:328
  130.2 0.8 copy.15
Async XLA Ops:
  2.6 1.3 copy-start
  3.8 1.3 copy-start.1
  5.1 1.1 copy-start.2
  6.2 1.1 copy-start.3
  7.2 1.1 copy-start.4
  8.3 0.8 copy-start.5
  9.2 0.8 copy-start.6
  10.0 0.7 copy-start.7
  10.7 0.7 copy-start.8
  11.4 0.7 copy-start.9

commit v2 on v1

--- a/solution.py
+++ b/solution.py
@@ -13,34 +13,33 @@
 SOFT_CAP = 50.0
 QUERY_SCALE = 144.0 ** (-0.5)
 MESH = pl.DeviceIdType.MESH
-CHUNKS = 4
+SIZES = (64, 32, 16, 16)
+CHUNKS = len(SIZES)
+STARTS = [sum(SIZES[:c]) for c in range(CHUNKS)]
 
 STEPS = [
-    ("A", 0, 0), ("D", 0), ("A", 1, 0),
-    ("U", 0, 0), ("A", 0, 1), ("U", 1, 0), ("U", 0, 1),
-    ("D", 1), ("A", 1, 1), ("U", 1, 1),
-    ("A", 0, 2), ("U", 0, 2), ("D", 2), ("X", 0), ("A", 1, 2), ("U", 1, 2),
-    ("A", 0, 3), ("A", 2, 0), ("U", 0, 3), ("D", 3), ("X", 1), ("A", 1, 3), ("U", 1, 3), ("A", 3, 0),
-    ("A", 0, 4), ("U", 0, 4), ("D", 4), ("A", 1, 4), ("U", 1, 4), ("U", 2, 0), ("U", 3, 0),
-    ("A", 2, 1), ("U", 2, 1), ("A", 3, 1), ("X", 2), ("U", 3, 1), ("A", 2, 2), ("X", 3),
-    ("U", 2, 2), ("A", 3, 2), ("U", 3, 2), ("W",), ("O", 0), ("A", 2, 3), ("U", 2, 3), ("O", 1), ("A", 3, 3), ("U", 3, 3),
-    ("A", 2, 4), ("U", 2, 4), ("A", 3, 4), ("U", 3, 4), ("O", 2), ("O", 3),
+    ("D", 0), ("A", 0, 0), ("D", 1), ("U", 0, 0), ("A", 0, 1), ("U", 1, 0), ("D", 2), ("X", 0), ("U", 2, 0),
+    ("A", 0, 2), ("D", 3), ("A", 1, 0), ("X", 1), ("U", 0, 2), ("U", 0, 1), ("U", 3, 0), ("D", 4), ("A", 0, 3),
+    ("A", 1, 1), ("U", 0, 3), ("A", 0, 4), ("X", 2), ("U", 0, 4), ("A", 2, 0), ("X", 3), ("U", 1, 1),
+    ("A", 1, 2), ("U", 1, 2), ("A", 3, 0), ("W",), ("A", 2, 1), ("O", 0), ("A", 1, 3), ("U", 1, 3), ("A", 3, 1),
+    ("U", 2, 1), ("A", 2, 2), ("A", 1, 4), ("U", 1, 4), ("U", 3, 1), ("A", 3, 2), ("U", 2, 2), ("A", 2, 3),
+    ("U", 2, 3), ("A", 3, 3), ("O", 1), ("A", 2, 4), ("U", 2, 4), ("U", 3, 3), ("A", 3, 4), ("U", 3, 4),
+    ("U", 3, 2), ("O", 2), ("O", 3),
 ]
 
 
 def kernel(
-    n_section, lens, x, gain_before, gain_after, cosine, sine, wq, wk, wv, wo,
+    n_section, lengths, order, fresh, x, gain_before, gain_after, cosine, sine, wq, wk, wv, wo,
     produced, received,
-    xg, wqkv, wout, keys, values, normed, outgoing, mixed, branch, made, g1, g2, cs, sn,
+    lens, chosen, pool, entering, xg, wqkv, wout, keys, values, normed, outgoing, mixed, branch, made, g1, g2, cs, sn,
     a_send, a_recv, d_send, d_recv, x_send, x_recv, e_send, e_recv, f_send, f_recv, c_send, c_recv,
-    z_send, z_recv, l_sem, o_sem,
+    z_send, z_recv, l_sem, o_sem, p_sem,
 ):
     n_tp = wout.shape[0]
     section = lax.axis_index("section")
     t = lax.axis_index("tp")
     dp = lax.axis_index("dp")
     seq, width = x.shape
-    rows = seq // CHUNKS
     group = wo.shape[0]
     quarter = group // 4
     kv = wk.shape[1]
@@ -50,13 +49,19 @@
     def at_tp(distance):
         return lax.rem(t + n_tp + distance, n_tp)
 
-    sources = (x, wq, wk, wv, wo, gain_before, gain_after, cosine, sine)
+    sources = (x, wq, wk, wv, wo, gain_before, gain_after, cosine, sine, lengths)
     targets = (
         xg.at[t], wqkv.at[:, :group], wqkv.at[:, group:group + kv], wqkv.at[:, group + kv:], wout.at[t], g1, g2, cs, sn,
+        lens,
     )
     local = [pltpu.make_async_copy(s, d, l_sem.at[i]) for i, (s, d) in enumerate(zip(sources, targets))]
     for copy in local:
         copy.start()
+
+    load_pool = [
+        pltpu.make_async_copy(fresh, pool, p_sem.at[0]), pltpu.make_async_copy(order, chosen, p_sem.at[1])
+    ]
+    enter = pltpu.make_async_copy(entering, received, p_sem.at[2])
 
     barrier = pltpu.get_barrier_semaphore()
     for distance in range(1, n_tp):
@@ -81,16 +86,18 @@
         copy.start()
         pending.append(copy)
 
-    def ring_rows(way, c, h):
-        if h < 3:
-            return pl.ds(c * rows, rows)
-        return pl.ds(c * rows + way * (rows // 2), rows // 2)
+    def part_of(c):
+        return slice(STARTS[c], STARTS[c] + SIZES[c])
+
+    def ring_part(way, c, h):
+        half = width // 2
+        return part_of(c), slice(0, width) if h < 3 else slice(way * half, (way + 1) * half)
 
     def ring(way, c, h, arriving):
         sign = 1 if way == 0 else -1
         block = at_tp(-sign * (h + 1 if arriving else h))
-        part = xg.at[block, ring_rows(way, c, h)]
-        src = x.at[ring_rows(way, c, h)] if h == 0 and not arriving else part
+        part = xg.at[(block, *ring_part(way, c, h))]
+        src = x.at[part_of(c)] if h == 0 and not arriving else part
         return remote(src, part, a_send.at[way, c, h], a_recv.at[way, c, h], {"tp": at_tp(sign)})
 
     def weight_rows(who, way, h):
@@ -118,10 +125,10 @@
         return remote(part, part, sems[0].at[way, h], sems[1].at[way, h], {"dp": other_core})
 
     def exchange(c, r):
-        return remote(outgoing.at[c, r], mixed.at[c, t], c_send.at[c, r], c_recv.at[c, r], {"tp": at_tp(r)})
+        return remote(outgoing.at[r, part_of(c)], mixed.at[t, part_of(c)], c_send.at[c, r], c_recv.at[c, r], {"tp": at_tp(r)})
 
     def exchange_arriving(c, r):
-        part = mixed.at[c, at_tp(-r)]
+        part = mixed.at[at_tp(-r), part_of(c)]
         return remote(part, part, c_send.at[c, r], c_recv.at[c, r], {"tp": at_tp(r)})
 
     late = []
@@ -131,6 +138,7 @@
             start(late.pop(0))
 
     def attend(c, g):
+        rows, at = SIZES[c], part_of(c)
         if g == 0:
             blocks = [(t, None)]
         elif g == n_tp // 2:
@@ -139,27 +147,27 @@
             blocks = [(at_tp(-g), n_tp - g), (at_tp(g), g)]
         gain = g1[...]
         for i, (block, _) in enumerate(blocks):
-            row = x_rows = xg[block, c * rows:(c + 1) * rows].astype(jnp.float32)
-            scale = lax.rsqrt(jnp.mean(row * row, -1, keepdims=True) + EPSILON)
-            normed[i * rows:(i + 1) * rows] = (x_rows * scale * gain).astype(jnp.bfloat16)
+            held = xg[block, at].astype(jnp.float32)
+            scale = lax.rsqrt(jnp.mean(held * held, -1, keepdims=True) + EPSILON)
+            normed[i * rows:(i + 1) * rows] = (held * scale * gain).astype(jnp.bfloat16)
         total = len(blocks) * rows
         projected = jnp.dot(normed[:total], wqkv[...], preferred_element_type=jnp.float32)
-        cos_part = cs[c * rows:(c + 1) * rows]
-        sin_part = sn[c * rows:(c + 1) * rows]
+        cos_part = cs[at]
+        sin_part = sn[at]
 
         def rotate(part):
             return (part * cos_part + pltpu.roll(part, HEAD_WIDTH // 2, 1) * sin_part).astype(jnp.bfloat16)
 
         heads = group // HEAD_WIDTH
-        query_at = lax.broadcasted_iota(jnp.int32, (heads * rows, seq), 0) % rows + c * rows
+        query_at = lax.broadcasted_iota(jnp.int32, (heads * rows, seq), 0) % rows + STARTS[c]
         key_at = lax.broadcasted_iota(jnp.int32, (heads * rows, seq), 1)
         for i, (block, r) in enumerate(blocks):
             part = projected[i * rows:(i + 1) * rows]
             query = jnp.concatenate(
                 [rotate(part[:, h * HEAD_WIDTH:(h + 1) * HEAD_WIDTH]) for h in range(heads)], 0
             )
-            keys[block, c * rows:(c + 1) * rows] = rotate(part[:, group:group + kv])
-            values[block, c * rows:(c + 1) * rows] = part[:, group + kv:].astype(jnp.bfloat16)
+            keys[block, at] = rotate(part[:, group:group + kv])
+            values[block, at] = part[:, group + kv:].astype(jnp.bfloat16)
             scores = lax.dot_general(
                 query, keys[block], (((1,), (1,)), ((), ())), preferred_element_type=jnp.float32
             )
@@ -171,13 +179,14 @@
             for h in range(heads):
                 piece = out[h * rows:(h + 1) * rows]
                 if r is None:
-                    mixed[c, t, :, h * HEAD_WIDTH:(h + 1) * HEAD_WIDTH] = piece
+                    mixed[t, at, h * HEAD_WIDTH:(h + 1) * HEAD_WIDTH] = piece
                 else:
-                    outgoing[c, r, :, h * HEAD_WIDTH:(h + 1) * HEAD_WIDTH] = piece
+                    outgoing[r, at, h * HEAD_WIDTH:(h + 1) * HEAD_WIDTH] = piece
             if r is not None:
                 late.append(exchange(c, r))
 
     def finish(c):
+        rows, part = SIZES[c], part_of(c)
         for r in range(1, n_tp):
             exchange_arriving(c, r).wait_recv()
         tile = 256
@@ -186,13 +195,12 @@
             cols = slice(n * tile, (n + 1) * tile)
             acc = jnp.zeros((rows, tile), jnp.float32)
             for j in range(n_tp):
-                acc += jnp.dot(mixed[c, j], wout[j, :, cols], preferred_element_type=jnp.float32)
-            branch[:, cols] = acc
+                acc += jnp.dot(mixed[j, part], wout[j, :, cols], preferred_element_type=jnp.float32)
+            branch[:rows, cols] = acc
             square += jnp.sum(acc * acc, -1, keepdims=True)
         scale = lax.rsqrt(square / width + EPSILON)
-        part = slice(c * rows, (c + 1) * rows)
         held = xg[t, part].astype(jnp.float32)
-        made[part] = (held + branch[...] * scale * g2[...]).astype(jnp.bfloat16)
+        made[part] = (held + branch[:rows] * scale * g2[...]).astype(jnp.bfloat16)
         copy = pltpu.make_async_copy(made.at[part], produced.at[part], o_sem.at[c])
         copy.start()
 
@@ -201,7 +209,7 @@
             send_on(c).start()
 
     def send_on(c):
-        part = slice(c * rows, (c + 1) * rows)
+        part = part_of(c)
         return remote(made.at[part], received.at[part], z_send.at[c], z_recv.at[c], {"section": section + 1})
 
     ready = False
@@ -233,6 +241,13 @@
                 start(weight_core(beside, way, h, True))
             flush()
         elif kind == "W":
+            @pl.when(section == 0)
+            def _():
+                for copy in load_pool:
+                    copy.wait()
+                entering[...] = pool[chosen[0]]
+                enter.start()
+
             for h in range(4):
                 for way in (0, 1):
                     weight_core(other_core, way, h, False).wait_recv()
@@ -243,17 +258,27 @@
                 values[...] = jnp.zeros_like(values)
                 for copy in local:
                     copy.wait()
+
+                @pl.when(section == 0)
+                def _():
+                    for copy in load_pool:
+                        copy.start()
+
                 ready = True
             flush()
             attend(step[1], step[2])
         else:
             flush()
             finish(step[1])
+
+    @pl.when(section == 0)
+    def _():
+        enter.wait()
 
     for copy in pending:
         copy.wait_send()
     for c in range(CHUNKS):
-        part = slice(c * rows, (c + 1) * rows)
+        part = part_of(c)
         pltpu.make_async_copy(made.at[part], produced.at[part], o_sem.at[c]).wait()
 
     @pl.when(section < n_section - 1)
@@ -284,7 +309,6 @@
 ):
     held = incoming[0, 0]
     seq, width = held.shape
-    rows = seq // CHUNKS
     wq, wk, wv, wo = w_query[0], key_weight[0], value_weight[0], w_out[0]
     group, kv = wq.shape[1], wk.shape[1]
     cosine, sine = tables(seq)
@@ -294,18 +318,22 @@
     produced, received = pl.pallas_call(
         functools.partial(kernel, n_section),
         out_shape=[jax.ShapeDtypeStruct((seq, width), bf16)] * 2,
-        in_specs=[pl.BlockSpec(memory_space=pltpu.SMEM)] + [hbm] * 9,
+        in_specs=[hbm] * 12,
         out_specs=[hbm] * 2,
         scratch_shapes=[
+            pltpu.SMEM(flight_lengths.shape, jnp.int32),
+            pltpu.SMEM(entry_order.shape, jnp.int32),
+            pltpu.VMEM((fresh_rows.shape[0], seq, width), bf16),
+            pltpu.VMEM((seq, width), bf16),
             pltpu.VMEM((n_tp, seq, width), bf16),
             pltpu.VMEM((width, group + 2 * kv), bf16),
             pltpu.VMEM((n_tp, group, width), bf16),
             pltpu.VMEM((n_tp, seq, kv), bf16),
             pltpu.VMEM((n_tp, seq, kv), bf16),
-            pltpu.VMEM((2 * rows, width), bf16),
-            pltpu.VMEM((CHUNKS, n_tp, rows, group), bf16),
-            pltpu.VMEM((CHUNKS, n_tp, rows, group), bf16),
-            pltpu.VMEM((rows, width), f32),
+            pltpu.VMEM((2 * max(SIZES), width), bf16),
+            pltpu.VMEM((n_tp, seq, group), bf16),
+            pltpu.VMEM((n_tp, seq, group), bf16),
+            pltpu.VMEM((max(SIZES), width), f32),
             pltpu.VMEM((seq, width), bf16),
             pltpu.VMEM((1, width), f32),
             pltpu.VMEM((1, width), f32),
@@ -314,18 +342,16 @@
             dma((2, CHUNKS, 4)), dma((2, CHUNKS, 4)),
             dma((2, 4)), dma((2, 4)), dma((2, 4)), dma((2, 4)), dma((2, 4)), dma((2, 4)), dma((2, 4)), dma((2, 4)),
             dma((CHUNKS, n_tp)), dma((CHUNKS, n_tp)),
-            dma((CHUNKS,)), dma((CHUNKS,)), dma((9,)), dma((CHUNKS,)),
+            dma((CHUNKS,)), dma((CHUNKS,)), dma((10,)), dma((CHUNKS,)), dma((3,)),
         ],
         compiler_params=pltpu.CompilerParams(
-            collective_id=0, has_side_effects=True, vmem_limit_bytes=40 * 1024 * 1024
+            collective_id=0, has_side_effects=True, vmem_limit_bytes=67043328
         ),
         name="relay",
     )(
-        flight_lengths, held, pre_gain, post_gain, jnp.asarray(cosine), jnp.asarray(sine), wq, wk, wv, wo,
-    )
-    entering = lax.dynamic_index_in_dim(fresh_rows, entry_order[0], 0, keepdims=False)[0]
-    advanced = jnp.where(lax.axis_index("section") == 0, entering, received)
-    return produced[None, None], advanced[None, None]
+        flight_lengths, entry_order, fresh_rows[:, 0], held, pre_gain, post_gain, jnp.asarray(cosine), jnp.asarray(sine), wq, wk, wv, wo,
+    )
+    return produced[None, None], received[None, None]
 
 
 def solution(mesh):

time: 132 us -> 120 us (0.909)
  local copies, waits for them, and re-layouts: 10.3 us -> 2.8 us
  between operations: 2.6 us -> 0.65 us
  other arithmetic: 1.95 us -> 0 us
    unnamed x21 -> x4, local copies, waits for them, and re-layouts: 10.3 us -> 2.8 us
    broadcast_in_dim x1 -> x0, other arithmetic: 1.95 us -> none  [shards(): return (produced[None, None], advanced[None, None])]
where the time goes in v2:
time: 120 us
  Pallas kernels  116 us (97%)
  local copies, waits for them, and re-layouts  2.8 us (2%)
    pallas_call x1, Pallas kernels, shards(): pl.pallas_call(functools.partial(kernel, n_section), out_shape=[jax.Shape...  116 us
    unnamed x4, local copies, waits for them, and re-layouts  2.8 us

profile of v2, /device:TPU:6, one launch (start us, length us, event | category | flops | bytes accessed | tf_op | source)
XLA Modules:
  0.0 119.5 jit_solution(16453375218874897941)
XLA Ops:
  0.6 116.1 %relay.1 = (bf16[128,2304]{1,0:T(8,128)(2,1)}, bf16[128,2304]{1,0:T(8,128)(2,1)}) custom-call(s32[1,8]{1,0:T(1,128)} %lengths.1, s32[6]{0:T(128)} %order.1, bf16[6,128,2304]{2,1,0:T(8,128)(2,1)} %bitcast.8, bf16[128,2304]{1,0:T(8,128)(2,1)} %bitcast.11, f32[1,2304]{1,0:T(1,128)} %gain_before.1, f32[1,2304]{1,0:T(1,128)} %gain_after.1, ...), custom_call_target="tpu_custom_call" | custom-call | tf_op jit(solution)/shard_map/relay/pallas_call | solution.py:318
  116.7 0.0 copy-start
  116.7 2.0 %copy.16 = bf16[1,1,128,2304]{3,2,1,0:T(8,128)(2,1)} copy(bf16[1,1,128,2304]{3,2,1,0:T(8,128)(2,1)} %bitcast.15) | data formatting | bytes 1179648
  118.7 0.0 copy-done
  118.7 0.8 copy.17
Async XLA Ops:
  116.7 2.0 %copy-start = (bf16[128,2304]{1,0:T(8,128)(2,1)S(1)}, bf16[128,2304]{1,0:T(8,128)(2,1)}, u32[]{:S(2)}) copy-start(bf16[128,2304]{1,0:T(8,128)(2,1)} %get-tuple-element.5) | copy-start | bytes 1769476

commit v3 on v2

--- a/solution.py
+++ b/solution.py
@@ -13,18 +13,19 @@
 SOFT_CAP = 50.0
 QUERY_SCALE = 144.0 ** (-0.5)
 MESH = pl.DeviceIdType.MESH
-SIZES = (64, 32, 16, 16)
+SIZES = (48, 32, 16, 16, 16)
 CHUNKS = len(SIZES)
 STARTS = [sum(SIZES[:c]) for c in range(CHUNKS)]
 
 STEPS = [
-    ("D", 0), ("A", 0, 0), ("D", 1), ("U", 0, 0), ("A", 0, 1), ("U", 1, 0), ("D", 2), ("X", 0), ("U", 2, 0),
-    ("A", 0, 2), ("D", 3), ("A", 1, 0), ("X", 1), ("U", 0, 2), ("U", 0, 1), ("U", 3, 0), ("D", 4), ("A", 0, 3),
-    ("A", 1, 1), ("U", 0, 3), ("A", 0, 4), ("X", 2), ("U", 0, 4), ("A", 2, 0), ("X", 3), ("U", 1, 1),
-    ("A", 1, 2), ("U", 1, 2), ("A", 3, 0), ("W",), ("A", 2, 1), ("O", 0), ("A", 1, 3), ("U", 1, 3), ("A", 3, 1),
-    ("U", 2, 1), ("A", 2, 2), ("A", 1, 4), ("U", 1, 4), ("U", 3, 1), ("A", 3, 2), ("U", 2, 2), ("A", 2, 3),
-    ("U", 2, 3), ("A", 3, 3), ("O", 1), ("A", 2, 4), ("U", 2, 4), ("U", 3, 3), ("A", 3, 4), ("U", 3, 4),
-    ("U", 3, 2), ("O", 2), ("O", 3),
+    ("D", 0), ("A", 0, 0), ("D", 1), ("A", 0, 1), ("D", 2), ("X", 0), ("A", 1, 0), ("D", 3), ("A", 2, 0),
+    ("A", 0, 2), ("U", 0, 0), ("U", 0, 2), ("A", 1, 1), ("X", 1), ("A", 3, 0), ("A", 0, 3), ("U", 1, 0),
+    ("D", 4), ("A", 2, 1), ("A", 1, 2), ("X", 2), ("U", 2, 0), ("U", 0, 3), ("A", 0, 4), ("U", 3, 0),
+    ("U", 0, 4), ("U", 0, 1), ("A", 4, 0), ("X", 3), ("A", 1, 3), ("A", 2, 2), ("W",), ("A", 4, 1), ("O", 0),
+    ("A", 1, 4), ("A", 3, 1), ("U", 1, 3), ("U", 1, 4), ("U", 1, 2), ("A", 2, 3), ("U", 4, 0), ("U", 1, 1),
+    ("A", 3, 2), ("A", 4, 2), ("U", 2, 2), ("U", 2, 3), ("A", 2, 4), ("U", 2, 4), ("O", 1), ("A", 3, 3),
+    ("U", 2, 1), ("U", 3, 1), ("A", 4, 3), ("U", 3, 3), ("U", 4, 3), ("A", 3, 4), ("U", 3, 4), ("U", 3, 2),
+    ("A", 4, 4), ("U", 4, 4), ("O", 2), ("U", 4, 2), ("U", 4, 1), ("O", 3), ("O", 4),
 ]
 
 

time: 120 us -> 125 us (1.042)
  Pallas kernels: 116 us -> 121 us
    pallas_call x1, Pallas kernels: 116 us -> 121 us  [shards(): pl.pallas_call(functools.partial(kernel, n_section), out_shape=[jax.Shape...]
where the time goes in v3:
time: 125 us
  Pallas kernels  121 us (97%)
  local copies, waits for them, and re-layouts  2.8 us (2%)
    pallas_call x1, Pallas kernels, shards(): pl.pallas_call(functools.partial(kernel, n_section), out_shape=[jax.Shape...  121 us
    unnamed x4, local copies, waits for them, and re-layouts  2.8 us

profile of v3, /device:TPU:6, one launch (start us, length us, event | category | flops | bytes accessed | tf_op | source)
XLA Modules:
  0.0 124.7 jit_solution(8129846431079162365)
XLA Ops:
  0.6 121.3 %relay.1 = (bf16[128,2304]{1,0:T(8,128)(2,1)}, bf16[128,2304]{1,0:T(8,128)(2,1)}) custom-call(s32[1,8]{1,0:T(1,128)} %lengths.1, s32[6]{0:T(128)} %order.1, bf16[6,128,2304]{2,1,0:T(8,128)(2,1)} %bitcast.8, bf16[128,2304]{1,0:T(8,128)(2,1)} %bitcast.11, f32[1,2304]{1,0:T(1,128)} %gain_before.1, f32[1,2304]{1,0:T(1,128)} %gain_after.1, ...), custom_call_target="tpu_custom_call" | custom-call | tf_op jit(solution)/shard_map/relay/pallas_call | solution.py:319
  121.9 0.0 copy-start
  121.9 2.0 %copy.16 = bf16[1,1,128,2304]{3,2,1,0:T(8,128)(2,1)} copy(bf16[1,1,128,2304]{3,2,1,0:T(8,128)(2,1)} %bitcast.15) | data formatting | bytes 1179648
  123.9 0.0 copy-done
  123.9 0.8 copy.17
Async XLA Ops:
  121.9 2.0 %copy-start = (bf16[128,2304]{1,0:T(8,128)(2,1)S(1)}, bf16[128,2304]{1,0:T(8,128)(2,1)}, u32[]{:S(2)}) copy-start(bf16[128,2304]{1,0:T(8,128)(2,1)} %get-tuple-element.5) | copy-start | bytes 1769476

commit v4 on v2

--- a/solution.py
+++ b/solution.py
@@ -13,18 +13,16 @@
 SOFT_CAP = 50.0
 QUERY_SCALE = 144.0 ** (-0.5)
 MESH = pl.DeviceIdType.MESH
-SIZES = (64, 32, 16, 16)
+SIZES = (64, 48, 16)
 CHUNKS = len(SIZES)
 STARTS = [sum(SIZES[:c]) for c in range(CHUNKS)]
 
 STEPS = [
-    ("D", 0), ("A", 0, 0), ("D", 1), ("U", 0, 0), ("A", 0, 1), ("U", 1, 0), ("D", 2), ("X", 0), ("U", 2, 0),
-    ("A", 0, 2), ("D", 3), ("A", 1, 0), ("X", 1), ("U", 0, 2), ("U", 0, 1), ("U", 3, 0), ("D", 4), ("A", 0, 3),
-    ("A", 1, 1), ("U", 0, 3), ("A", 0, 4), ("X", 2), ("U", 0, 4), ("A", 2, 0), ("X", 3), ("U", 1, 1),
-    ("A", 1, 2), ("U", 1, 2), ("A", 3, 0), ("W",), ("A", 2, 1), ("O", 0), ("A", 1, 3), ("U", 1, 3), ("A", 3, 1),
-    ("U", 2, 1), ("A", 2, 2), ("A", 1, 4), ("U", 1, 4), ("U", 3, 1), ("A", 3, 2), ("U", 2, 2), ("A", 2, 3),
-    ("U", 2, 3), ("A", 3, 3), ("O", 1), ("A", 2, 4), ("U", 2, 4), ("U", 3, 3), ("A", 3, 4), ("U", 3, 4),
-    ("U", 3, 2), ("O", 2), ("O", 3),
+    ("D", 0), ("U", 0, 0), ("U", 1, 0), ("A", 0, 0), ("D", 1), ("A", 0, 1), ("D", 2), ("X", 0), ("A", 0, 2),
+    ("U", 0, 1), ("D", 3), ("U", 2, 0), ("X", 1), ("A", 1, 0), ("D", 4), ("A", 0, 3), ("U", 0, 3), ("A", 1, 1),
+    ("X", 2), ("U", 0, 2), ("X", 3), ("A", 0, 4), ("U", 0, 4), ("A", 1, 2), ("A", 2, 0), ("W",), ("U", 1, 2),
+    ("O", 0), ("A", 1, 3), ("A", 2, 1), ("U", 1, 3), ("A", 1, 4), ("U", 1, 4), ("A", 2, 2), ("U", 1, 1),
+    ("U", 2, 2), ("A", 2, 3), ("O", 1), ("A", 2, 4), ("U", 2, 4), ("U", 2, 3), ("U", 2, 1), ("O", 2),
 ]
 
 

time: 120 us -> 125 us (1.042)
  Pallas kernels: 116 us -> 122 us
    pallas_call x1, Pallas kernels: 116 us -> 122 us  [shards(): pl.pallas_call(functools.partial(kernel, n_section), out_shape=[jax.Shape...]
where the time goes in v4:
time: 125 us
  Pallas kernels  122 us (98%)
  local copies, waits for them, and re-layouts  2.8 us (2%)
    pallas_call x1, Pallas kernels, shards(): pl.pallas_call(functools.partial(kernel, n_section), out_shape=[jax.Shape...  122 us
    unnamed x4, local copies, waits for them, and re-layouts  2.8 us

profile of v4, /device:TPU:6, one launch (start us, length us, event | category | flops | bytes accessed | tf_op | source)
XLA Modules:
  0.0 125.0 jit_solution(5209911599374986689)
XLA Ops:
  0.6 121.5 %relay.1 = (bf16[128,2304]{1,0:T(8,128)(2,1)}, bf16[128,2304]{1,0:T(8,128)(2,1)}) custom-call(s32[1,8]{1,0:T(1,128)} %lengths.1, s32[6]{0:T(128)} %order.1, bf16[6,128,2304]{2,1,0:T(8,128)(2,1)} %bitcast.8, bf16[128,2304]{1,0:T(8,128)(2,1)} %bitcast.11, f32[1,2304]{1,0:T(1,128)} %gain_before.1, f32[1,2304]{1,0:T(1,128)} %gain_after.1, ...), custom_call_target="tpu_custom_call" | custom-call | tf_op jit(solution)/shard_map/relay/pallas_call | solution.py:316
  122.1 0.0 copy-start
  122.2 2.0 %copy.16 = bf16[1,1,128,2304]{3,2,1,0:T(8,128)(2,1)} copy(bf16[1,1,128,2304]{3,2,1,0:T(8,128)(2,1)} %bitcast.15) | data formatting | bytes 1179648
  124.1 0.0 copy-done
  124.1 0.8 copy.17
Async XLA Ops:
  122.1 2.0 %copy-start = (bf16[128,2304]{1,0:T(8,128)(2,1)S(1)}, bf16[128,2304]{1,0:T(8,128)(2,1)}, u32[]{:S(2)}) copy-start(bf16[128,2304]{1,0:T(8,128)(2,1)} %get-tuple-element.5) | copy-start | bytes 1769476
